TPU v7x, 32 devices: a whole 2x2x4 slice. The times are simulated.
32 devices in a mesh: band: 8 (over z, y), head: 4 (over x, core).
Axes of the slice: x: 2, y: 2, z: 4, core: 2. Of those that a mesh axis runs over, the one named last changes fastest.
Arguments:
- grid_feat: bfloat16 [65536, 1024], P(('band', 'head')), may hold values from -7 to 7
- mesh_feat: bfloat16 [4096, 1024], P(('band', 'head')), may hold values from -7 to 7
- enc_query: bfloat16 [1024, 1024], replicated, may hold values from -0.1875 to 0.1875
- enc_keyval: bfloat16 [1024, 2048], replicated, may hold values from -0.1875 to 0.1875
- enc_out: bfloat16 [1024, 1024], replicated, may hold values from -0.1875 to 0.1875
- proc_qkv: bfloat16 [3, 1024, 1024], P(None, None, 'head'), may hold values from -0.1875 to 0.1875
- proc_out: bfloat16 [1024, 1024], P('head'), may hold values from -0.1875 to 0.1875
- tile_ids: int32 [64, 8], P(('band', 'head')), may hold values from 0 to 511, as said below
- key_counts: int32 [64], P(('band', 'head')), may hold values from 128 to 1024, as said below
Outputs:
- mesh_out: bfloat16 [4096, 1024], P(('band', 'head'))
Inputs may be any that keep to these rules, and one draw needn't show every extreme that they name: `tile_ids`: mesh tile m lies on the device that holds mesh rows m * 64; every tile it lists is one of that device's grid tiles (grid rows of the same device) or of the 2 grid tiles just before or just after them. Slots may repeat tiles. `key_counts`: the largest value is reached in every draw.
All inputs are finite; a program needn't handle non-finite values.
Results may differ from a plain program's by a relative error of at most 0.012.
The roundings to bfloat16 on the way count: a program that leaves them out, or rounds other values in their place, can miss the bound.
Values may be sent and summed in bfloat16 or wider, within the bound.
A program may use at most 128 MiB of HBM per device.

v0:
```python
import math

import jax
import jax.numpy as jnp
from jax import lax
from jax.sharding import PartitionSpec as P

D = 1024
HEADS = 16
HALFW = 512
GT = 128
LIST = 8
MT = 64
HALO_TILES = 2


def extended(shard, sides, width):
    for axis, dim in sides:
        size, length = (lax.axis_size(axis), shard.shape[dim])
        up = [(i, (i + 1) % size) for i in range(size - 1)]
        down = [(j, i) for i, j in up]
        last = lax.slice_in_dim(shard, length - width, length, axis=dim)
        first = lax.slice_in_dim(shard, 0, width, axis=dim)
        before = lax.ppermute(last, axis, up)
        after = lax.ppermute(first, axis, down)
        shard = jnp.concatenate([before, shard, after], axis=dim)
    return shard


def masked_softmax(scores, key_mask):
    scores = jnp.where(key_mask, scores, -1e30)
    row_top = jnp.max(scores, axis=-1, keepdims=True)
    weights = jnp.exp(scores - row_top)
    return (weights / jnp.sum(weights, axis=-1, keepdims=True)).astype(jnp.bfloat16)


def local(
    grid_feat, mesh_feat, enc_query, enc_keyval, enc_out, proc_qkv, proc_out, tile_ids, key_counts
):
    grid_count, model_width = grid_feat.shape
    mesh_count = mesh_feat.shape[0]
    tiles_dev = grid_count // GT
    head_size = D // HEADS
    score_scale = head_size ** (-0.5)
    device = lax.axis_index(("band", "head"))
    grid_kv = jnp.dot(grid_feat, enc_keyval, preferred_element_type=jnp.float32).astype(
        jnp.bfloat16
    )
    bordered = extended(
        grid_kv.reshape(tiles_dev, GT * 2 * model_width), ((("band", "head"), 0),), HALO_TILES
    )
    grid_tiles = bordered.reshape(-1, GT, 2 * model_width)
    queries = jnp.dot(mesh_feat, enc_query, preferred_element_type=jnp.float32).astype(jnp.bfloat16)
    local_lists = tile_ids - (device * tiles_dev - HALO_TILES)
    positions = jnp.arange(LIST * GT, dtype=jnp.int32)

    def one_tile(packed):
        query_tile, tile_list, valid = packed
        gathered = grid_tiles[tile_list].reshape(LIST * GT, 2 * model_width)
        key_rows = gathered[:, :model_width].reshape(LIST * GT, HEADS, head_size)
        value_rows = gathered[:, model_width:].reshape(LIST * GT, HEADS, head_size)
        query_heads = query_tile.reshape(MT, HEADS, head_size)
        scores = (
            jnp.einsum("qhd,khd->hqk", query_heads, key_rows, preferred_element_type=jnp.float32)
            * score_scale
        )
        weights = masked_softmax(scores, (positions < valid)[None, None, :])
        attended = jnp.einsum(
            "hqk,khd->qhd", weights, value_rows, preferred_element_type=jnp.float32
        )
        return attended.reshape(MT, model_width).astype(jnp.bfloat16)

    enc_attn = lax.map(
        one_tile, (queries.reshape(mesh_count // MT, MT, model_width), local_lists, key_counts)
    )
    enc_attn = enc_attn.reshape(mesh_count, model_width)
    mesh_state = (
        mesh_feat.astype(jnp.float32)
        + jnp.dot(enc_attn, enc_out, preferred_element_type=jnp.float32)
    ).astype(jnp.bfloat16)
    head_cols = proc_qkv.shape[2]
    piece = lax.all_gather(mesh_state, "head", axis=0, tiled=True)
    product = jnp.einsum("rd,tdc->rtc", piece, proc_qkv, preferred_element_type=jnp.float32)
    projected = product.astype(jnp.bfloat16).reshape(piece.shape[0], 3 * head_cols)
    group_rows = projected.shape[0]
    bordered_kv = extended(projected[:, head_cols:], (("band", 0),), HALFW)
    local_heads = head_cols // head_size
    block_rows = math.gcd(group_rows, 512)
    band_start = lax.axis_index("band") * group_rows
    mesh_total = group_rows * lax.axis_size("band")

    def one_block(block_index):
        first = block_index * block_rows
        span = block_rows + 2 * HALFW
        query_heads = lax.dynamic_slice_in_dim(projected, first, block_rows, 0)[
            :, :head_cols
        ].reshape(block_rows, local_heads, head_size)
        window_rows = lax.dynamic_slice_in_dim(bordered_kv, first, span, 0)
        key_rows = window_rows[:, :head_cols].reshape(span, local_heads, head_size)
        value_rows = window_rows[:, head_cols:].reshape(span, local_heads, head_size)
        query_pos = band_start + first + jnp.arange(block_rows, dtype=jnp.int32)
        key_pos = band_start + first - HALFW + jnp.arange(span, dtype=jnp.int32)
        near = (jnp.abs(query_pos[:, None] - key_pos[None, :]) < HALFW) & (
            (key_pos >= 0) & (key_pos < mesh_total)
        )[None, :]
        scores = (
            jnp.einsum("qhd,khd->hqk", query_heads, key_rows, preferred_element_type=jnp.float32)
            * score_scale
        )
        weights = masked_softmax(scores, near[None, :, :])
        attended = jnp.einsum(
            "hqk,khd->qhd", weights, value_rows, preferred_element_type=jnp.float32
        )
        return attended.reshape(block_rows, head_cols).astype(jnp.bfloat16)

    proc_attn = lax.map(one_block, jnp.arange(group_rows // block_rows, dtype=jnp.int32)).reshape(
        group_rows, head_cols
    )
    own_rows = lax.all_to_all(proc_attn, "head", split_axis=0, concat_axis=1, tiled=True)
    out_weights = lax.all_gather(proc_out, "head", axis=0, tiled=True)
    head_total = jnp.dot(own_rows, out_weights, preferred_element_type=jnp.float32)
    return (mesh_state.astype(jnp.float32) + head_total).astype(jnp.bfloat16)


def solution(mesh):
    return jax.shard_map(
        local,
        mesh=mesh,
        in_specs=(
            P(("band", "head"), None),
            P(("band", "head"), None),
            P(),
            P(),
            P(),
            P(None, None, "head"),
            P("head", None),
            P(("band", "head"), None),
            P(("band", "head")),
        ),
        out_specs=P(("band", "head"), None),
        check_vma=False,
    )
```

profile of v0, /device:TPU:22, one launch (start us, length us, event | category | flops | bytes accessed | tf_op | source)
XLA Modules:
  0.0 206.5 jit_solution(7345442903268691120)
XLA Ops:
  6.5 12.1 %convolution_convert_fusion = bf16[2048,2048]{1,0:T(8,128)(2,1)S(1)} fusion(bf16[2048,1024]{1,0:T(8,128)(2,1)} %param.11, bf16[1024,2048]{1,0:T(8,128)(2,1)} %param.14), kind=kOutput, calls=%fused_computation.30 | convolution fusion | flops 8594128896 | bytes 16777216 | tf_op jit(solution)/shard_map/dot_general | solution.py:46
  18.6 3.3 %copy-done.3 = bf16[2048,2048]{1,0:T(8,128)(2,1)} copy-done((bf16[2048,2048]{1,0:T(8,128)(2,1)}, bf16[2048,2048]{1,0:T(8,128)(2,1)S(1)}, u32[]{:S(2)}) %copy-start.3) | copy-done | bytes 8388632
  23.1 3.0 %slice.36 = bf16[2,262144]{1,0:T(2,128)(2,1)} reshape(bf16[256,2048]{1,0:T(8,128)(2,1)} %get-tuple-element.89) | data formatting | bytes 2097152 | tf_op jit(solution)/shard_map/slice | solution.py:23
  32.9 19.0 %collective-permute-done.1 = bf16[2,262144]{1,0:T(2,128)(2,1)} collective-permute-done((bf16[2,262144]{1,0:T(2,128)(2,1)}, bf16[2,262144]{1,0:T(2,128)(2,1)}, u32[]{:S(2)}, u32[]{:S(2)}) %collective-permute-start.1) | collective-permute-done | bytes 1048608 | tf_op jit(solution)/shard_map/ppermute | solution.py:25
  55.3 10.7 %pad_maximum_fusion = bf16[20,128,2048]{2,1,0:T(8,128)(2,1)} fusion(bf16[2,128,2048]{2,1,0:T(8,128)(2,1)S(1)} %bitcast.79, bf16[16,128,2048]{2,1,0:T(8,128)(2,1)} %bitcast.77, bf16[2,128,2048]{2,1,0:T(8,128)(2,1)S(1)} %bitcast.80), kind=kLoop, calls=%fused_computation.28 | loop fusion | flops 10485760 | bytes 20971520 | tf_op jit(solution)/shard_map/concatenate | solution.py:26
  66.0 52.4 %while.3 = (s32[]{:T(128)}, bf16[2,64,1024]{2,1,0:T(8,128)(2,1)S(1)}, s32[2,8]{1,0:T(2,128)S(1)}, bf16[20,128,2048]{2,1,0:T(8,128)(2,1)}, s32[2]{0:T(128)S(1)}, /*index=5*/bf16[2,64,1024]{2,1,0:T(8,128)(2,1)S(1)}, s32[]{:T(128)}) while((s32[]{:T(128)}, bf16[2,64,1024]{2,1,0:T(8,128)(2,1)S(1)}, s32[2,8]{1,0:T(2,128)S(1)}, ...), condition=%wide.region_3.4_spmd.clone, body=%wide.region_0.3_spmd.clone.sunk | while | flops 276892704 | bytes 55851268 | solution.py:73
  66.0 6.8 %gather_fusion = bf16[8,128,2048]{2,1,0:T(8,128)(2,1)} fusion(bf16[20,128,2048]{2,1,0:T(8,128)(2,1)} %get-tuple-element.156, s32[1024]{0:T(1024)S(1)} %pad_clamp_fusion.2), kind=kCustom, calls=%fused_computation.clone.clone.1 | custom fusion | bytes 8388640 | tf_op jit(solution)/shard_map/while/body/eval_jaxpr/gather | solution.py:59
  72.9 4.6 %fusion.64 = (bf16[1024,1024]{1,0:T(8,128)(2,1)}, bf16[1024,1024]{1,0:T(8,128)(2,1)}) fusion(bf16[1024,2048]{1,0:T(8,128)(2,1)} %bitcast.74), kind=kLoop, calls=%fused_computation.56.clone.1 | loop fusion | bytes 8388608 | tf_op jit(solution)/shard_map/while/body/eval_jaxpr/slice | solution.py:60
  77.5 2.9 %copy.38 = bf16[1024,1024]{0,1:T(8,128)(2,1)S(1)} copy(bf16[1024,1024]{1,0:T(8,128)(2,1)} %get-tuple-element.136) | data formatting | bytes 4194304 | tf_op jit(solution)/shard_map/while
  82.5 3.3 %fusion.66 = (f32[16,64]{1,0:T(8,128)S(1)}, f32[16,64,1024]{2,1,0:T(8,128)}) fusion(f32[16,64,1024]{2,1,0:T(8,128)S(1)} %fusion.65, pred[1024]{0:T(1024)(128)(4,1)S(1)} %iota_compare_fusion.2), kind=kOutput, calls=%fused_computation.57.clone.1 | output fusion | flops 6292479 | bytes 8393728 | tf_op jit(solution)/shard_map/while/body/eval_jaxpr/sub | solution.py:33
  88.4 3.6 %fusion.67 = bf16[16,64,64]{2,1,0:T(8,128)(2,1)S(1)} fusion(bf16[1024,16,64]{0,2,1:T(8,128)(2,1)} %bitcast.76, f32[16,64,1024]{2,1,0:T(8,128)} %get-tuple-element.137, f32[16,64]{1,0:T(8,128)S(1)} %get-tuple-element.138), kind=kOutput, calls=%fused_computation.11.clone.1 | convolution fusion | flops 136380416 | bytes 6426624 | tf_op jit(solution)/shard_map/while/body/eval_jaxpr/hqk,khd->qhd/dot_general | solution.py:68
  92.2 6.8 %gather_fusion = bf16[8,128,2048]{2,1,0:T(8,128)(2,1)} fusion(bf16[20,128,2048]{2,1,0:T(8,128)(2,1)} %get-tuple-element.156, s32[1024]{0:T(1024)S(1)} %pad_clamp_fusion.2), kind=kCustom, calls=%fused_computation.clone.clone.1 | custom fusion | bytes 8388640 | tf_op jit(solution)/shard_map/while/body/eval_jaxpr/gather | solution.py:59
  99.1 4.6 %fusion.64 = (bf16[1024,1024]{1,0:T(8,128)(2,1)}, bf16[1024,1024]{1,0:T(8,128)(2,1)}) fusion(bf16[1024,2048]{1,0:T(8,128)(2,1)} %bitcast.74), kind=kLoop, calls=%fused_computation.56.clone.1 | loop fusion | bytes 8388608 | tf_op jit(solution)/shard_map/while/body/eval_jaxpr/slice | solution.py:60
  103.7 2.9 %copy.38 = bf16[1024,1024]{0,1:T(8,128)(2,1)S(1)} copy(bf16[1024,1024]{1,0:T(8,128)(2,1)} %get-tuple-element.136) | data formatting | bytes 4194304 | tf_op jit(solution)/shard_map/while
  108.7 3.3 %fusion.66 = (f32[16,64]{1,0:T(8,128)S(1)}, f32[16,64,1024]{2,1,0:T(8,128)}) fusion(f32[16,64,1024]{2,1,0:T(8,128)S(1)} %fusion.65, pred[1024]{0:T(1024)(128)(4,1)S(1)} %iota_compare_fusion.2), kind=kOutput, calls=%fused_computation.57.clone.1 | output fusion | flops 6292479 | bytes 8393728 | tf_op jit(solution)/shard_map/while/body/eval_jaxpr/sub | solution.py:33
  114.6 3.6 %fusion.67 = bf16[16,64,64]{2,1,0:T(8,128)(2,1)S(1)} fusion(bf16[1024,16,64]{0,2,1:T(8,128)(2,1)} %bitcast.76, f32[16,64,1024]{2,1,0:T(8,128)} %get-tuple-element.137, f32[16,64]{1,0:T(8,128)S(1)} %get-tuple-element.138), kind=kOutput, calls=%fused_computation.11.clone.1 | convolution fusion | flops 136380416 | bytes 6426624 | tf_op jit(solution)/shard_map/while/body/eval_jaxpr/hqk,khd->qhd/dot_general | solution.py:68
  122.0 16.6 %all-gather.3.cloned.1.call-done = bf16[512,1024]{1,0:T(8,128)(2,1)} async-done(((bf16[128,1024]{1,0:T(8,128)(2,1)}), bf16[512,1024]{1,0:T(8,128)(2,1)}) %all-gather.3.cloned.1.call-update) | async-done | bytes 1048592 | tf_op jit(solution)/shard_map/all_gather | solution.py:82
  141.4 3.4 %collective-permute-start.2 = (bf16[512,512]{0,1:T(8,128)(2,1)S(1)}, bf16[512,512]{0,1:T(8,128)(2,1)S(1)}, u32[]{:S(2)}, u32[]{:S(2)}) collective-permute-start(bf16[512,512]{0,1:T(8,128)(2,1)S(1)} %slice.49), channel_id=1, source_target_pairs={{0,4},{4,8},{8,12},{12,16},{16,20},{20,24},{24,28},{1,5},{5,9},{9,... | collective-permute-start | bytes 1572872 | tf_op jit(solution)/shard_map/ppermute | solution.py:24
  148.5 20.1 %collective-permute-done.2 = bf16[512,512]{0,1:T(8,128)(2,1)S(1)} collective-permute-done((bf16[512,512]{0,1:T(8,128)(2,1)S(1)}, bf16[512,512]{0,1:T(8,128)(2,1)S(1)}, u32[]{:S(2)}, u32[]{:S(2)}) %collective-permute-start.2) | collective-permute-done | bytes 524320 | tf_op jit(solution)/shard_map/ppermute | solution.py:24
  170.0 9.8 %fusion.35 = (f32[4,512]{1,0:T(4,128)S(1)}, f32[4,512,1536]{2,1,0:T(8,128)}) fusion(pred[512,1536]{1,0:T(8,128)(4,1)S(1)} %fusion.21, bf16[512,4,64]{0,2,1:T(8,128)(2,1)S(1)} %bitcast.87, bf16[1536,4,64]{0,2,1:T(8,128)(2,1)} %bitcast.86), kind=kOutput, calls=%fused_computation.60 | convolution fusion | flops 415237632 | bytes 14426112 | tf_op jit(solution)/shard_map/while/body/eval_jaxpr/sub | solution.py:33
  179.8 7.0 %fusion.25 = bf16[512,4,64]{0,2,1:T(8,128)(2,1)S(1)} fusion(bf16[1536,4,64]{0,2,1:T(8,128)(2,1)} %bitcast.85, f32[4,512,1536]{2,1,0:T(8,128)} %get-tuple-element.93, f32[4,512]{1,0:T(4,128)S(1)} %get-tuple-element.92), kind=kOutput, calls=%fused_computation.45 | convolution fusion | flops 409075712 | bytes 13639680 | tf_op jit(solution)/shard_map/while/body/eval_jaxpr/hqk,khd->qhd/dot_general | solution.py:111
  187.7 4.8 %all-to-all-start = ((bf16[4,128,256]{1,2,0:T(8,128)(2,1)}), bf16[4,128,256]{1,2,0:T(8,128)(2,1)S(1)}, u32[]{:S(2)}, u32[]{:S(2)}) async-start(bf16[4,128,256]{1,2,0:T(8,128)(2,1)} %copy.18), calls=%async_computation | async-start | bytes 524288 | tf_op jit(solution)/shard_map/all_to_all | solution.py:119
  192.5 4.4 %all-to-all-done = bf16[4,128,256]{1,2,0:T(8,128)(2,1)S(1)} async-done(((bf16[4,128,256]{1,2,0:T(8,128)(2,1)}), bf16[4,128,256]{1,2,0:T(8,128)(2,1)S(1)}, u32[]{:S(2)}, u32[]{:S(2)}) %all-to-all-start) | async-done | bytes 262176 | tf_op jit(solution)/shard_map/all_to_all | solution.py:119
  196.9 2.8 %fusion.24 = bf16[128,1024]{1,0:T(8,128)(2,1)} fusion(bf16[128,1024]{0,1:T(8,128)(2,1)S(1)} %bitcast.82, bf16[1024,1024]{1,0:T(8,128)(2,1)} %all-gather.5.cloned.1.call-done, bf16[128,1024]{1,0:T(8,128)(2,1)S(1)} %copy-done.4), kind=kOutput, calls=%fused_computation.44 | convolution fusion | flops 268828672 | bytes 2883584 | tf_op jit(solution)/shard_map/dot_general | solution.py:121
  (66 shorter events, 33.2 us)
Async XLA Ops:
  6.5 25.9 %copy-start = (bf16[1024,1024]{1,0:T(8,128)(2,1)S(1)}, bf16[1024,1024]{1,0:T(8,128)(2,1)}, u32[]{:S(2)}) copy-start(bf16[1024,1024]{1,0:T(8,128)(2,1)} %param.13) | copy-start | bytes 6291460
  6.5 132.1 %all-gather.3.cloned.1.call-start = ((), (), s32[]{:S(2)}) async-start(), calls=%async_computation.1 | async-start | bytes 1310720 | tf_op jit(solution)/shard_map/all_gather | solution.py:82
  18.6 3.3 %copy-start.3 = (bf16[2048,2048]{1,0:T(8,128)(2,1)}, bf16[2048,2048]{1,0:T(8,128)(2,1)S(1)}, u32[]{:S(2)}) copy-start(bf16[2048,2048]{1,0:T(8,128)(2,1)S(1)} %convolution_convert_fusion) | copy-start | bytes 25165828
  21.9 10.4 %copy-start.6 = (s32[2,8]{1,0:T(2,128)S(1)}, s32[2,8]{1,0:T(2,128)}, u32[]{:S(2)}) copy-start(s32[2,8]{1,0:T(2,128)} %param.18) | copy-start | bytes 196
  21.9 10.5 %copy-start.5 = (bf16[128,1024]{1,0:T(8,128)(2,1)S(1)}, bf16[128,1024]{1,0:T(8,128)(2,1)}, u32[]{:S(2)}) copy-start(bf16[128,1024]{1,0:T(8,128)(2,1)} %param.12) | copy-start | bytes 786436
  26.1 25.8 %collective-permute-start.1 = (bf16[2,262144]{1,0:T(2,128)(2,1)}, bf16[2,262144]{1,0:T(2,128)(2,1)}, u32[]{:S(2)}, u32[]{:S(2)}) collective-permute-start(bf16[2,262144]{1,0:T(2,128)(2,1)} %slice.36), channel_id=1, source_target_pairs={{1,0},{2,1},{3,2},{4,3},{5,4},{6,5},{7,6},{8,7},{9,8},{10,9},{11,1... | collective-permute-start | bytes 3145736 | tf_op jit(solution)/shard_map/ppermute | solution.py:25
  29.8 24.0 %collective-permute-start = (bf16[2,262144]{1,0:T(2,128)(2,1)}, bf16[2,262144]{1,0:T(2,128)(2,1)}, u32[]{:S(2)}, u32[]{:S(2)}) collective-permute-start(bf16[2,262144]{1,0:T(2,128)(2,1)} %slice.34), channel_id=1, source_target_pairs={{0,1},{1,2},{2,3},{3,4},{4,5},{5,6},{6,7},{7,8},{8,9},{9,10},{10,1... | collective-permute-start | bytes 3145736 | tf_op jit(solution)/shard_map/ppermute | solution.py:24
  55.3 10.7 %copy-start.7 = (s32[2]{0:T(128)S(1)}, s32[2]{0:T(128)}, u32[]{:S(2)}) copy-start(s32[2]{0:T(128)} %param.19) | copy-start | bytes 28
  82.5 3.3 %copy-start.2 = (bf16[1024,1024]{1,0:T(8,128)(2,1)S(1)}, bf16[1024,1024]{1,0:T(8,128)(2,1)}, u32[]{:S(2)}) copy-start(bf16[1024,1024]{1,0:T(8,128)(2,1)} %get-tuple-element.135) | copy-start | bytes 6291460 | tf_op jit(solution)/shard_map/while
  108.7 3.3 %copy-start.2 = (bf16[1024,1024]{1,0:T(8,128)(2,1)S(1)}, bf16[1024,1024]{1,0:T(8,128)(2,1)}, u32[]{:S(2)}) copy-start(bf16[1024,1024]{1,0:T(8,128)(2,1)} %get-tuple-element.135) | copy-start | bytes 6291460 | tf_op jit(solution)/shard_map/while
  121.2 71.3 %all-gather.5.cloned.1.call-start = ((), (), s32[]{:S(2)}) async-start(), calls=%async_computation.2 | async-start | bytes 2621440 | tf_op jit(solution)/shard_map/all_gather | solution.py:120
  141.4 27.2 %collective-permute-start.2 = (bf16[512,512]{0,1:T(8,128)(2,1)S(1)}, bf16[512,512]{0,1:T(8,128)(2,1)S(1)}, u32[]{:S(2)}, u32[]{:S(2)}) collective-permute-start(bf16[512,512]{0,1:T(8,128)(2,1)S(1)} %slice.49), channel_id=1, source_target_pairs={{0,4},{4,8},{8,12},{12,16},{16,20},{20,24},{24,28},{1,5},{5,9},{9,... | collective-permute-start | bytes 1572872 | tf_op jit(solution)/shard_map/ppermute | solution.py:24
  144.8 23.8 %collective-permute-start.3 = (bf16[512,512]{0,1:T(8,128)(2,1)S(1)}, bf16[512,512]{0,1:T(8,128)(2,1)S(1)}, u32[]{:S(2)}, u32[]{:S(2)}) collective-permute-start(bf16[512,512]{0,1:T(8,128)(2,1)S(1)} %slice.49), channel_id=1, source_target_pairs={{4,0},{8,4},{12,8},{16,12},{20,16},{24,20},{28,24},{5,1},{9,5},{13... | collective-permute-start | bytes 1572872 | tf_op jit(solution)/shard_map/ppermute | solution.py:25
  179.8 17.1 %copy-start.4 = (bf16[128,1024]{1,0:T(8,128)(2,1)S(1)}, bf16[128,1024]{1,0:T(8,128)(2,1)}, u32[]{:S(2)}) copy-start(bf16[128,1024]{1,0:T(8,128)(2,1)} %fusion.23) | copy-start | bytes 786436
  179.8 19.8 %copy-start.1 = (bf16[1024,1024]{1,0:T(8,128)(2,1)S(1)}, bf16[1024,1024]{1,0:T(8,128)(2,1)}, u32[]{:S(2)}) copy-start(bf16[1024,1024]{1,0:T(8,128)(2,1)} %param.13) | copy-start | bytes 6291460
  187.7 9.2 %all-to-all-start = ((bf16[4,128,256]{1,2,0:T(8,128)(2,1)}), bf16[4,128,256]{1,2,0:T(8,128)(2,1)S(1)}, u32[]{:S(2)}, u32[]{:S(2)}) async-start(bf16[4,128,256]{1,2,0:T(8,128)(2,1)} %copy.18), calls=%async_computation | async-start | bytes 524288 | tf_op jit(solution)/shard_map/all_to_all | solution.py:119
Sparse Core Ops, SparseCore 0:
  121.3 17.2 all-gather.2
  140.1 22.5 all-gather.4
where the time goes:
time: 209 us; the launch traced here: 206 us
  waiting for transfers between devices  61.1 us (29%)
  local copies, waits for them, and re-layouts  50.2 us (24%)
  matrix products  46.2 us (22%)
  other arithmetic  19.7 us (9%)
  starting transfers between devices  15.4 us (7%)
  between operations  13.6 us (7%)
    ppermute x2, waiting for transfers between devices, extended(): before = lax.ppermute(last, axis, up)  20.4 us
    ppermute x2, waiting for transfers between devices, extended(): after = lax.ppermute(first, axis, down)  19 us
    all_gather x1, waiting for transfers between devices, local(): piece = lax.all_gather(mesh_state, 'head', axis=0, tiled=True)  16.6 us
    gather x2, local copies, waits for them, and re-layouts, one_tile(): gathered = grid_tiles[tile_list].reshape(LIST * GT, 2 * model_width)  13.7 us
    dot_general x1, matrix products, local(): jnp.dot(grid_feat, enc_keyval, preferred_element_type=jnp.float32)  12.1 us
    while x8, local copies, waits for them, and re-layouts  10.9 us
    concatenate x2, other arithmetic, extended(): shard = jnp.concatenate([before, shard, after], axis=dim)  10.8 us
    sub x1, matrix products, masked_softmax(): weights = jnp.exp(scores - row_top)  9.83 us
  transfers between devices with their start and end apart: 7, of which 5 were waited for; matrix products, arithmetic and copies ran while one was open for 13% of the time, Pallas kernels for 0%

commit v1 on v0

v1 whole, which is shorter than its diff:
```python
import functools

import jax
import jax.numpy as jnp
from jax import lax
from jax.experimental import pallas as pl
from jax.experimental.pallas import tpu as pltpu
from jax.sharding import PartitionSpec as P

HEADS = 16
HALFW = 512
GT = 128
MT = 64
HALO_TILES = 2
BF = jnp.bfloat16
F32 = jnp.float32
MESH_ID = pl.DeviceIdType.MESH
NEG = -1e30


def dot(a, b):
    return jnp.dot(a, b, preferred_element_type=F32)


def dot_t(a, b):
    return lax.dot_general(a, b, (((1,), (1,)), ((), ())), preferred_element_type=F32)


def pair_rows(q2, half):
    lane = lax.broadcasted_iota(jnp.int32, q2.shape, 1)
    low = lane < half
    zero = jnp.zeros_like(q2)
    return jnp.concatenate([jnp.where(low, q2, zero), jnp.where(low, zero, q2)], axis=0)


def pair_merge(o2, rows, half):
    lane = lax.broadcasted_iota(jnp.int32, (rows, 2 * half), 1)
    return jnp.where(lane < half, o2[:rows], o2[rows:])


def softmax_rows(scores):
    top = jnp.max(scores, axis=-1, keepdims=True)
    weights = jnp.exp(scores - top)
    return (weights * (1.0 / jnp.sum(weights, axis=-1, keepdims=True))).astype(BF)


def kernel(
    nb, nh, tid, cnt, grid, feat_h, wquery_h, wkv_h, wenc_h, qkv_h, pout_h, out,
    g, halo, wkv, wquery, wenc, feat, kv, wq, wo, st, qs, att, kp, vp, bias,
    lsem, hs_send, hs_recv,
    wp_send, wp_recv, wx_send, wx_recv, wy_send, wy_recv, wf_send, wf_recv, wg_send, wg_recv,
    s_send, s_recv, f_send,
):
    n = nb * nh
    band = lax.axis_index("band")
    head = lax.axis_index("head")
    d = band * nh + head
    core = lax.rem(head, 2)
    par = lax.rem(band, 2)
    mate = head + 1 - 2 * core
    twin = band + 1 - 2 * par
    xs = nh // 2
    rows, dm = feat.shape
    tiles = grid.shape[0] // GT
    edge = HALO_TILES * GT
    cols = qkv_h.shape[2]
    slots = st.shape[0]
    reach = slots // 2
    head_size = dm // HEADS
    pairs = HEADS // 2
    wide = 2 * head_size
    scale = head_size ** (-0.5)

    def flat_id(f):
        return (f // nh, lax.rem(f, nh))

    def remote(src, dst, ss, rs, dev):
        return pltpu.make_async_remote_copy(
            src_ref=src, dst_ref=dst, send_sem=ss, recv_sem=rs, device_id=dev,
            device_id_type=MESH_ID)

    gchunk = g.shape[0] // 4
    wchunk = wkv.shape[1] // 4
    local = []
    for i in range(4):
        local.append(pltpu.make_async_copy(
            wkv_h.at[:, pl.ds(i * wchunk, wchunk)], wkv.at[:, pl.ds(i * wchunk, wchunk)],
            lsem.at[i]))
        local.append(pltpu.make_async_copy(
            grid.at[pl.ds(i * gchunk, gchunk)], g.at[pl.ds(i * gchunk, gchunk)], lsem.at[4 + i]))
    local.append(pltpu.make_async_copy(feat_h, feat, lsem.at[8]))
    local.append(pltpu.make_async_copy(wquery_h, wquery, lsem.at[9]))
    local.append(pltpu.make_async_copy(wenc_h, wenc, lsem.at[10]))
    local.append(pltpu.make_async_copy(qkv_h, wq.at[head], lsem.at[11]))
    own_out = pl.multiple_of(head * cols, cols)
    local.append(pltpu.make_async_copy(pout_h, wo.at[pl.ds(own_out, cols)], lsem.at[12]))
    for c in local:
        c.start()

    bar = pltpu.get_barrier_semaphore()
    expect = jnp.int32(0)
    for off in (-4, -2, -1, 1, 2, 4):
        ok = (d + off >= 0) & (d + off < n)
        expect = expect + ok.astype(jnp.int32)

        @pl.when(ok)
        def _(off=off):
            pl.semaphore_signal(bar, inc=1, device_id=flat_id(d + off), device_id_type=MESH_ID)

    for k in range(1, xs):
        pl.semaphore_signal(bar, inc=1, device_id=(band, lax.rem(head + 2 * k, nh)),
                            device_id_type=MESH_ID)
    pl.semaphore_signal(bar, inc=1, device_id=(twin, head), device_id_type=MESH_ID)
    pl.semaphore_signal(bar, inc=1, device_id=(band, mate), device_id_type=MESH_ID)
    pl.semaphore_wait(bar, expect + (xs + 1))

    first, last = d == 0, d == n - 1
    up = remote(grid.at[pl.ds(grid.shape[0] - edge, edge)], halo.at[0], hs_send.at[0],
                hs_recv.at[0], flat_id(lax.rem(d + 1, n)))
    down = remote(grid.at[pl.ds(0, edge)], halo.at[1], hs_send.at[1], hs_recv.at[1],
                  flat_id(lax.rem(d + n - 1, n)))

    @pl.when(jnp.logical_not(last))
    def _():
        up.start()

    @pl.when(jnp.logical_not(first))
    def _():
        down.start()

    @pl.when(first)
    def _():
        halo[0] = jnp.zeros(halo.shape[1:], BF)

    @pl.when(last)
    def _():
        halo[1] = jnp.zeros(halo.shape[1:], BF)

    half = dm // 2
    ohalf = cols // 2

    def piece(p, src, y):
        if p < 3:
            t = (1, 2, 0)[p]
            return wq.at[src, t, pl.ds(pl.multiple_of(y * half, half), half)]
        return wo.at[pl.ds(pl.multiple_of(src * cols + y * ohalf, ohalf), ohalf)]

    def own_piece(p, y):
        if p < 3:
            t = (1, 2, 0)[p]
            return qkv_h.at[t, pl.ds(pl.multiple_of(y * half, half), half)]
        return pout_h.at[pl.ds(pl.multiple_of(y * ohalf, ohalf), ohalf)]

    def full_piece(p, src):
        if p < 3:
            return wq.at[src, (1, 2, 0)[p]]
        return wo.at[pl.ds(pl.multiple_of(src * cols, cols), cols)]

    def own_full(p):
        return qkv_h.at[(1, 2, 0)[p]] if p < 3 else pout_h

    def src_of(h, k):
        return lax.rem(h - 2 * k + nh, nh)

    def cross(p, k):
        return remote(own_piece(p, par), piece(p, head, par), wx_send.at[p, k - 1],
                      wx_recv.at[p, k - 1], (band, lax.rem(head + 2 * k, nh)))

    def to_mate(p):
        return remote(own_full(p), full_piece(p, head), wp_send.at[p], wp_recv.at[p], (band, mate))

    def relay(p, k, y, ss, rs, dev):
        src = src_of(head, k)
        return remote(piece(p, src, y), piece(p, src, y), ss.at[p, k - 1], rs.at[p, k - 1], dev)

    def to_twin(p, k):
        return relay(p, k, par, wy_send, wy_recv, (twin, head))

    def near_mate(p, k):
        return relay(p, k, par, wf_send, wf_recv, (band, mate))

    def far_mate(p, k):
        return relay(p, k, 1 - par, wg_send, wg_recv, (band, mate))

    for p in range(4):
        for k in range(1, xs):
            cross(p, k).start()
        to_mate(p).start()

    def stage_one(p):
        for k in range(1, xs):
            src = src_of(head, k)
            remote(own_piece(p, par), piece(p, src, par), wx_send.at[p, k - 1],
                   wx_recv.at[p, k - 1], (band, mate)).wait_recv()
            to_twin(p, k).start()
            near_mate(p, k).start()

    def stage_two(p):
        for k in range(1, xs):
            src = src_of(head, k)
            remote(own_piece(p, par), piece(p, src, 1 - par), wy_send.at[p, k - 1],
                   wy_recv.at[p, k - 1], (band, mate)).wait_recv()
            far_mate(p, k).start()

    def stage_three(p):
        remote(own_full(p), full_piece(p, mate), wp_send.at[p], wp_recv.at[p],
               (band, mate)).wait_recv()
        for k in range(1, xs):
            src = src_of(mate, k)
            for y, ss, rs in ((par, wf_send, wf_recv), (1 - par, wg_send, wg_recv)):
                remote(own_piece(p, y), piece(p, src, y), ss.at[p, k - 1], rs.at[p, k - 1],
                       (band, mate)).wait_recv()

    for e in range(slots):
        if e != reach:
            ok = (d - reach + e >= 0) & (d - reach + e < n)

            @pl.when(jnp.logical_not(ok))
            def _(e=e):
                st[e] = jnp.zeros(st.shape[1:], BF)

    brow = lax.broadcasted_iota(jnp.int32, (rows, slots * rows), 0)
    bcol = lax.broadcasted_iota(jnp.int32, (rows, slots * rows), 1)
    kpos = (d - reach) * rows + bcol
    near = (bcol - HALFW - brow < HALFW) & (bcol - HALFW - brow > -HALFW)
    near = near & (kpos >= 0) & (kpos < n * rows)
    bias[...] = jnp.where(near, 0.0, NEG).astype(F32)

    for i in range(4):
        local[2 * i].wait()
    for i in range(4):
        local[2 * i + 1].wait()
        ct = gchunk // GT

        def col_step(j, _, i=i, ct=ct):
            cs = pl.ds(pl.multiple_of(j * wchunk, wchunk), wchunk)
            r = dot(g[pl.ds(i * gchunk, gchunk)], wkv[:, cs]).astype(BF)
            kv[pl.ds(HALO_TILES + i * ct, ct), :, cs] = r.reshape(ct, GT, wchunk)
            return 0

        lax.fori_loop(0, 4, col_step, 0)
    local[8].wait()
    local[9].wait()
    local[10].wait()
    qs[...] = (dot(feat[...], wquery[...]).astype(BF) * scale).astype(BF)

    @pl.when(jnp.logical_not(first))
    def _():
        up.wait_recv()

    @pl.when(jnp.logical_not(last))
    def _():
        down.wait_recv()

    def halo_step(j, _):
        cs = pl.ds(pl.multiple_of(j * wchunk, wchunk), wchunk)
        r = dot(halo[...].reshape(2 * edge, dm), wkv[:, cs]).astype(BF)
        r = r.reshape(2 * HALO_TILES, GT, wchunk)
        kv[pl.ds(0, HALO_TILES), :, cs] = r[:HALO_TILES]
        kv[pl.ds(HALO_TILES + tiles, HALO_TILES), :, cs] = r[HALO_TILES:]
        return 0

    lax.fori_loop(0, 4, halo_step, 0)
    stage_one(0)

    base = d * tiles - HALO_TILES
    lists = tid.shape[1]
    for m in range(rows // MT):
        ids = [jnp.clip(tid[m, s] - base, 0, kv.shape[0] - 1) for s in range(lists)]
        valid = cnt[m]

        def pair_step(j, _, m=m, ids=ids, valid=valid):
            cs = pl.ds(pl.multiple_of(j * wide, wide), wide)
            vs = pl.ds(pl.multiple_of(dm + j * wide, wide), wide)
            q2 = pair_rows(qs[pl.ds(m * MT, MT), cs], head_size)
            k2 = jnp.concatenate([kv[t, :, cs] for t in ids], axis=0)
            scores = dot_t(q2, k2)
            pos = lax.broadcasted_iota(jnp.int32, scores.shape, 1)
            w = softmax_rows(jnp.where(pos < valid, scores, NEG))
            v2 = jnp.concatenate([kv[t, :, vs] for t in ids], axis=0)
            att[pl.ds(m * MT, MT), cs] = pair_merge(dot(w, v2), MT, head_size).astype(BF)
            return 0

        lax.fori_loop(0, pairs, pair_step, 0)
        if m == 0:
            stage_one(1)
    st[reach] = (feat[...].astype(F32) + dot(att[...], wenc[...])).astype(BF)

    mate_slot = reach + 1 - 2 * core

    def state_to(i, off):
        return remote(st.at[reach], st.at[reach - off], s_send.at[i], s_recv.at[reach - off],
                      flat_id(lax.rem(d + off + n, n)))

    offs = (2, -2, 4, -4)
    mate_copy = remote(st.at[reach], st.at[reach - 1 + 2 * core], s_send.at[4],
                       s_recv.at[reach - 1 + 2 * core], (band, mate))
    mate_copy.start()
    for i, off in enumerate(offs):
        @pl.when((d + off >= 0) & (d + off < n))
        def _(i=i, off=off):
            state_to(i, off).start()

    stage_one(2)
    stage_two(0)
    stage_two(1)
    local[11].wait()
    local[12].wait()
    stage_three(0)
    stage_three(1)

    def project(e):
        def step(h, _):
            cs = pl.ds(pl.multiple_of(h * cols, cols), cols)
            rs = pl.ds(pl.multiple_of(e * rows, rows), rows)
            x = st[e]
            kp[rs, cs] = dot(x, wq[h, 1]).astype(BF)
            vp[rs, cs] = dot(x, wq[h, 2]).astype(BF)
            return 0

        lax.fori_loop(0, nh, step, 0)

    def in_range(e):
        return (d - reach + e >= 0) & (d - reach + e < n)

    def wait_slot(e):
        @pl.when(in_range(e))
        def _():
            remote(st.at[reach], st.at[e], s_send.at[4], s_recv.at[e], (band, mate)).wait_recv()

    def pass_on(i, e):
        to = e - 1 + 2 * core
        return remote(st.at[e], st.at[to], f_send.at[i], s_recv.at[to], (band, mate))

    def passes(e):
        ok = in_range(e)
        if e == 0:
            ok = ok & (core == 1)
        if e == slots - 1:
            ok = ok & (core == 0)
        return ok

    def receive(i, e):
        wait_slot(e)

        @pl.when(passes(e))
        def _():
            pass_on(i, e).start()

    project(reach)
    stage_one(3)
    wait_slot(mate_slot)
    project(mate_slot)
    stage_two(2)
    receive(0, 2)
    receive(1, 6)
    project(2)
    stage_three(2)

    def query_step(h, _):
        cs = pl.ds(pl.multiple_of(h * cols, cols), cols)
        qs[:, cs] = (dot(st[reach], wq[h, 0]).astype(BF) * scale).astype(BF)
        return 0

    lax.fori_loop(0, nh, query_step, 0)
    receive(2, 0)
    receive(3, 8)
    project(6)
    project(0)
    project(8)
    far_slot = reach - 1 + 2 * core
    for e in (far_slot, 1, 7):
        wait_slot(e)
        project(e)
    stage_two(3)

    def window_step(j, _):
        cs = pl.ds(pl.multiple_of(j * wide, wide), wide)
        q2 = pair_rows(qs[:, cs], head_size)
        scores = dot_t(q2, kp[:, cs])
        b = bias[...]
        w = softmax_rows(scores + jnp.concatenate([b, b], axis=0))
        att[:, cs] = pair_merge(dot(w, vp[:, cs]), rows, head_size).astype(BF)
        return 0

    lax.fori_loop(0, pairs, window_step, 0)
    stage_three(3)
    out[...] = (st[reach].astype(F32) + dot(att[...], wo[...])).astype(BF)

    @pl.when(jnp.logical_not(last))
    def _():
        up.wait_send()

    @pl.when(jnp.logical_not(first))
    def _():
        down.wait_send()

    for p in range(4):
        to_mate(p).wait_send()
        for k in range(1, xs):
            cross(p, k).wait_send()
            to_twin(p, k).wait_send()
            near_mate(p, k).wait_send()
            far_mate(p, k).wait_send()
    mate_copy.wait_send()
    for i, off in enumerate(offs):
        @pl.when((d + off >= 0) & (d + off < n))
        def _(i=i, off=off):
            state_to(i, off).wait_send()

    for i, e in enumerate((2, 6, 0, 8)):
        @pl.when(passes(e))
        def _(i=i, e=e):
            pass_on(i, e).wait_send()


def local(nb, nh, grid_feat, mesh_feat, enc_query, enc_keyval, enc_out, proc_qkv, proc_out,
          tile_ids, key_counts):
    rows, dm = mesh_feat.shape
    grows = grid_feat.shape[0]
    tiles = grows // GT + 2 * HALO_TILES
    slots = 2 * (HALFW // rows) + 1
    cols = proc_qkv.shape[2]
    xs = nh // 2
    dma = pltpu.SemaphoreType.DMA
    any_spec = pl.BlockSpec(memory_space=pl.ANY)
    smem = pl.BlockSpec(memory_space=pltpu.SMEM)
    pieces = (4, max(xs - 1, 1))
    return pl.pallas_call(
        functools.partial(kernel, nb, nh),
        out_shape=jax.ShapeDtypeStruct((rows, dm), BF),
        in_specs=[smem, smem] + [any_spec] * 7,
        out_specs=pl.BlockSpec(memory_space=pltpu.VMEM),
        scratch_shapes=[
            pltpu.VMEM((grows, dm), BF),
            pltpu.VMEM((2, HALO_TILES * GT, dm), BF),
            pltpu.VMEM(enc_keyval.shape, BF),
            pltpu.VMEM(enc_query.shape, BF),
            pltpu.VMEM(enc_out.shape, BF),
            pltpu.VMEM((rows, dm), BF),
            pltpu.VMEM((tiles, GT, 2 * dm), BF),
            pltpu.VMEM((nh, 3, dm, cols), BF),
            pltpu.VMEM((nh * cols, dm), BF),
            pltpu.VMEM((slots, rows, dm), BF),
            pltpu.VMEM((rows, dm), BF),
            pltpu.VMEM((rows, dm), BF),
            pltpu.VMEM((slots * rows, dm), BF),
            pltpu.VMEM((slots * rows, dm), BF),
            pltpu.VMEM((rows, slots * rows), F32),
            dma((13,)), dma((2,)), dma((2,)),
            dma((4,)), dma((4,)),
            dma(pieces), dma(pieces), dma(pieces), dma(pieces),
            dma(pieces), dma(pieces), dma(pieces), dma(pieces),
            dma((5,)), dma((slots,)), dma((4,)),
        ],
        compiler_params=pltpu.CompilerParams(
            collective_id=0, has_side_effects=True, vmem_limit_bytes=63 * 1024 * 1024),
    )(tile_ids, key_counts, grid_feat, mesh_feat, enc_query, enc_keyval, enc_out, proc_qkv,
      proc_out)


def solution(mesh):
    return jax.shard_map(
        functools.partial(local, mesh.shape["band"], mesh.shape["head"]),
        mesh=mesh,
        in_specs=(
            P(("band", "head"), None),
            P(("band", "head"), None),
            P(),
            P(),
            P(),
            P(None, None, "head"),
            P("head", None),
            P(("band", "head"), None),
            P(("band", "head")),
        ),
        out_specs=P(("band", "head"), None),
        check_vma=False,
    )
```

time: 209 us -> 84.6 us (0.40)
  the two profiles are of different devices: /device:TPU:22 before, /device:TPU:25 now
where the time goes in v1:
time: 84.6 us; the launch traced here: 84.4 us
  Pallas kernels  82.7 us (98%)
  local copies, waits for them, and re-layouts  1.67 us (2%)
    pallas_call x1, Pallas kernels, local(): pl.pallas_call(functools.partial(kernel, nb, nh), out_shape=jax.ShapeDtyp...  82.7 us

profile of v1, /device:TPU:25, one launch (start us, length us, event | category | flops | bytes accessed | tf_op | source)
XLA Modules:
  0.0 84.4 jit_solution(3642116905367274761)
XLA Ops:
  0.0 82.7 %shard_map.91 = bf16[128,1024]{1,0:T(8,128)(2,1)} custom-call(s32[2,8]{1,0:T(2,128)} %tid.1, s32[2]{0:T(128)} %cnt.1, bf16[2048,1024]{1,0:T(8,128)(2,1)} %grid.1, bf16[128,1024]{1,0:T(8,128)(2,1)} %feat_h.1, bf16[1024,1024]{1,0:T(8,128)(2,1)} %wquery_h.1, bf16[1024,2048]{1,0:T(8,128)(2,1)} %wkv_h.1, bf16[1024,1024]{1,0:T(8,128)(2,1)} %wenc_h.1, ...), custom_call_target="tpu_custom_call" | custom-call | tf_op jit(solution)/shard_map/pallas_call | solution.py:429
  82.7 1.7 %copy.11 = bf16[128,1024]{1,0:T(8,128)(2,1)} copy(bf16[128,1024]{1,0:T(8,128)(2,1)} %shard_map.91) | data formatting | bytes 524288

commit v2 on v1

v2 whole, which is shorter than its diff:
```python
import functools

import jax
import jax.numpy as jnp
from jax import lax
from jax.experimental import pallas as pl
from jax.experimental.pallas import tpu as pltpu
from jax.sharding import PartitionSpec as P

HEADS = 16
HALFW = 512
GT = 128
MT = 64
HALO_TILES = 2
BF = jnp.bfloat16
F32 = jnp.float32
MESH_ID = pl.DeviceIdType.MESH
NEG = -1e30
GROUP = 4


def dot(a, b):
    return jnp.dot(a, b, preferred_element_type=F32)


def dot_t(a, b):
    return lax.dot_general(a, b, (((1,), (1,)), ((), ())), preferred_element_type=F32)


def group_rows(q, count, width):
    lane = lax.broadcasted_iota(jnp.int32, q.shape, 1)
    zero = jnp.zeros_like(q)
    return jnp.concatenate(
        [jnp.where((lane >= i * width) & (lane < (i + 1) * width), q, zero)
         for i in range(count)], axis=0)


def group_merge(o, rows, count, width):
    lane = lax.broadcasted_iota(jnp.int32, (rows, count * width), 1)
    r = o[:rows]
    for i in range(1, count):
        r = jnp.where(lane < i * width, r, o[i * rows:(i + 1) * rows])
    return r


def softmax_rows(scores):
    top = jnp.max(scores, axis=-1, keepdims=True)
    weights = jnp.exp(scores - top)
    return (weights * (1.0 / jnp.sum(weights, axis=-1, keepdims=True))).astype(BF)


def kernel(
    nb, nh, tid, cnt, grid, feat_h, wquery_h, wkv_h, wenc_h, qkv_h, pout_h, out,
    g, halo, wkv, wquery, wenc, feat, kv, wq, wo, st, qs, att, qh, kp, vp, mine, got, bias,
    lsem, hs_send, hs_recv, w_send, w_recv, ox_send, ox_recv, op_send, op_recv,
    m_send, x_send, v_send, r_send, p_send, s_recv, a_send, a_recv,
):
    n = nb * nh
    band = lax.axis_index("band")
    head = lax.axis_index("head")
    d = band * nh + head
    core = lax.rem(head, 2)
    x = head // 2
    mate = head + 1 - 2 * core
    xs = nh // 2
    rows, dm = feat.shape
    tiles = grid.shape[0] // GT
    edge = HALO_TILES * GT
    cols = qkv_h.shape[2]
    slots = st.shape[0]
    reach = HALFW // rows
    hop = reach // 2
    halves = rows // MT
    head_size = dm // HEADS
    wide = GROUP * head_size
    scale = head_size ** (-0.5)

    def flat_id(f):
        return (f // nh, lax.rem(f, nh))

    def remote(src, dst, ss, rs, dev):
        return pltpu.make_async_remote_copy(
            src_ref=src, dst_ref=dst, send_sem=ss, recv_sem=rs, device_id=dev,
            device_id_type=MESH_ID)

    gchunk = g.shape[0] // 4
    wchunk = wkv.shape[1] // 4
    local = []
    for i in range(4):
        local.append(pltpu.make_async_copy(
            wkv_h.at[:, pl.ds(i * wchunk, wchunk)], wkv.at[:, pl.ds(i * wchunk, wchunk)],
            lsem.at[i]))
        local.append(pltpu.make_async_copy(
            grid.at[pl.ds(i * gchunk, gchunk)], g.at[pl.ds(i * gchunk, gchunk)], lsem.at[4 + i]))
    local.append(pltpu.make_async_copy(feat_h, feat, lsem.at[8]))
    local.append(pltpu.make_async_copy(wquery_h, wquery, lsem.at[9]))
    local.append(pltpu.make_async_copy(wenc_h, wenc, lsem.at[10]))
    local.append(pltpu.make_async_copy(qkv_h, wq.at[core], lsem.at[11]))

    def out_rows(src):
        return wo.at[pl.ds(pl.multiple_of(src * cols, cols), cols)]

    local.append(pltpu.make_async_copy(pout_h, out_rows(head), lsem.at[12]))
    for c in local:
        c.start()

    def same_core(k):
        return (band, lax.rem(head + 2 * k, nh))

    def same_core_src(h, k):
        return lax.rem(h - 2 * k + nh, nh)

    bar = pltpu.get_barrier_semaphore()
    expect = jnp.int32(0)
    for off in (-nh, -1, 1, nh):
        ok = (d + off >= 0) & (d + off < n)
        expect = expect + ok.astype(jnp.int32)

        @pl.when(ok)
        def _(off=off):
            pl.semaphore_signal(bar, inc=1, device_id=flat_id(d + off), device_id_type=MESH_ID)

    for k in range(1, xs):
        pl.semaphore_signal(bar, inc=1, device_id=same_core(k), device_id_type=MESH_ID)
    pl.semaphore_signal(bar, inc=1, device_id=(band, mate), device_id_type=MESH_ID)
    pl.semaphore_wait(bar, expect + xs)

    first, last = d == 0, d == n - 1
    up = remote(grid.at[pl.ds(grid.shape[0] - edge, edge)], halo.at[0], hs_send.at[0],
                hs_recv.at[0], flat_id(lax.rem(d + 1, n)))
    down = remote(grid.at[pl.ds(0, edge)], halo.at[1], hs_send.at[1], hs_recv.at[1],
                  flat_id(lax.rem(d + n - 1, n)))

    @pl.when(jnp.logical_not(last))
    def _():
        up.start()

    @pl.when(jnp.logical_not(first))
    def _():
        down.start()

    @pl.when(first)
    def _():
        halo[0] = jnp.zeros(halo.shape[1:], BF)

    @pl.when(last)
    def _():
        halo[1] = jnp.zeros(halo.shape[1:], BF)

    qkv_mate = remote(qkv_h, wq.at[core], w_send.at[0], w_recv.at[0], (band, mate))
    out_mate = remote(pout_h, out_rows(head), w_send.at[1], w_recv.at[1], (band, mate))

    def out_cross(k):
        return remote(pout_h, out_rows(head), ox_send.at[k - 1], ox_recv.at[k - 1], same_core(k))

    def out_pass(k):
        src = out_rows(same_core_src(head, k))
        return remote(src, src, op_send.at[k - 1], op_recv.at[k - 1], (band, mate))

    for k in range(1, xs):
        out_cross(k).start()
    qkv_mate.start()
    out_mate.start()

    below, above = band > 0, band < nb - 1
    for e in range(slots):
        if e < reach:
            ok = below
        elif e >= nh + reach:
            ok = above
        else:
            continue
        if e == 0:
            ok = ok & (core == 0)
        if e == slots - 1:
            ok = ok & (core == 1)

        @pl.when(jnp.logical_not(ok))
        def _(e=e):
            st[e] = jnp.zeros(st.shape[1:], BF)

    span = (2 * reach + 1) * rows
    brow = lax.broadcasted_iota(jnp.int32, (rows, span), 0)
    bcol = lax.broadcasted_iota(jnp.int32, (rows, span), 1)
    near = (bcol - HALFW - brow < HALFW) & (bcol - HALFW - brow > -HALFW)
    for q in range(xs):
        kpos = (band * nh + 2 * q + core - reach) * rows + bcol
        bias[q] = jnp.where(near & (kpos >= 0) & (kpos < n * rows), 0.0, NEG).astype(F32)

    for i in range(4):
        local[2 * i].wait()
    for i in range(4):
        local[2 * i + 1].wait()
        ct = gchunk // GT

        def col_step(j, _, i=i, ct=ct):
            cs = pl.ds(pl.multiple_of(j * wchunk, wchunk), wchunk)
            r = dot(g[pl.ds(i * gchunk, gchunk)], wkv[:, cs]).astype(BF)
            kv[pl.ds(HALO_TILES + i * ct, ct), :, cs] = r.reshape(ct, GT, wchunk)
            return 0

        lax.fori_loop(0, 4, col_step, 0)
    local[8].wait()
    local[9].wait()
    local[10].wait()
    qs[...] = (dot(feat[...], wquery[...]).astype(BF) * scale).astype(BF)

    @pl.when(jnp.logical_not(first))
    def _():
        up.wait_recv()

    @pl.when(jnp.logical_not(last))
    def _():
        down.wait_recv()

    def halo_step(j, _):
        cs = pl.ds(pl.multiple_of(j * wchunk, wchunk), wchunk)
        r = dot(halo[...].reshape(2 * edge, dm), wkv[:, cs]).astype(BF)
        r = r.reshape(2 * HALO_TILES, GT, wchunk)
        kv[pl.ds(0, HALO_TILES), :, cs] = r[:HALO_TILES]
        kv[pl.ds(HALO_TILES + tiles, HALO_TILES), :, cs] = r[HALO_TILES:]
        return 0

    lax.fori_loop(0, 4, halo_step, 0)

    own = head + reach
    to_above = above & (x >= xs - hop)
    to_below = below & (x < hop)

    def part(e, u):
        return st.at[e, pl.ds(u * MT, MT)]

    def state_mate(u):
        return remote(part(own, u), part(own, u), m_send.at[u], s_recv.at[own, u], (band, mate))

    def state_x(k, u):
        return remote(part(own, u), part(own, u), x_send.at[k - 1, u], s_recv.at[own, u],
                      same_core(k))

    def state_v(i, u):
        sign = 1 - 2 * i
        to = own - sign * nh
        to = jnp.clip(to, 0, slots - 1)
        dev = (jnp.clip(band + sign, 0, nb - 1), head)
        return remote(part(own, u), part(to, u), v_send.at[i, u], s_recv.at[to, u], dev)

    base = d * tiles - HALO_TILES
    lists = tid.shape[1]
    for m in range(halves):
        ids = [jnp.clip(tid[m, s] - base, 0, kv.shape[0] - 1) for s in range(lists)]
        valid = cnt[m]

        def group_step(j, _, m=m, ids=ids, valid=valid):
            cs = pl.ds(pl.multiple_of(j * wide, wide), wide)
            vs = pl.ds(pl.multiple_of(dm + j * wide, wide), wide)
            q2 = group_rows(qs[pl.ds(m * MT, MT), cs], GROUP, head_size)
            k2 = jnp.concatenate([kv[t, :, cs] for t in ids], axis=0)
            scores = dot_t(q2, k2)
            pos = lax.broadcasted_iota(jnp.int32, scores.shape, 1)
            w = softmax_rows(jnp.where(pos < valid, scores, NEG))
            v2 = jnp.concatenate([kv[t, :, vs] for t in ids], axis=0)
            att[pl.ds(m * MT, MT), cs] = group_merge(dot(w, v2), MT, GROUP, head_size).astype(BF)
            return 0

        lax.fori_loop(0, HEADS // GROUP, group_step, 0, unroll=2)
        ms = pl.ds(m * MT, MT)
        st[own, ms] = (feat[ms].astype(F32) + dot(att[ms], wenc[...])).astype(BF)
        for k in range(1, xs):
            state_x(k, m).start()
        for i, ok in enumerate((to_above, to_below)):
            @pl.when(ok)
            def _(i=i, m=m):
                state_v(i, m).start()
        state_mate(m).start()

    def arrived(e, u):
        remote(part(own, u), part(e, u), m_send.at[u], s_recv.at[e, u], (band, mate)).wait_recv()

    def slot_of(j):
        return 2 * j + core

    def mate_slot(j):
        return 2 * j + 1 - core

    def hand(j, u):
        e = slot_of(j)
        return remote(part(e, u), part(e, u), p_send.at[j, u], s_recv.at[e, u], (band, mate))

    def wanted(j):
        e = slot_of(j)
        return (e >= 1 - core) & (e <= slots - 1 - core)

    def relay(i, k, j, u):
        e = slot_of(j)
        return remote(part(e, u), part(e, u), r_send.at[i, k - 1, u], s_recv.at[e, u],
                      same_core(k))

    def project(j):
        def step(h, _):
            cs = pl.ds(pl.multiple_of(h * cols, cols), cols)
            rs = pl.ds(pl.multiple_of(j * 2 * rows, 2 * rows), 2 * rows)
            y = st[pl.ds(2 * j, 2)].reshape(2 * rows, dm)
            kp[rs, cs] = dot(y, wq[h, 1]).astype(BF)
            vp[rs, cs] = dot(y, wq[h, 2]).astype(BF)
            return 0

        lax.fori_loop(0, 2, step, 0)

    def from_mate(j):
        e = mate_slot(j)
        ok = (e >= core) & (e <= slots - 2 + core)
        if isinstance(j, int):
            if j < hop:
                ok = ok & below
            elif j >= xs + hop:
                ok = ok & above
        else:
            ok = ok & ((j >= hop) | below) & ((j < xs + hop) | above)

        @pl.when(ok)
        def _():
            for u in range(halves):
                arrived(e, u)

    def query(q):
        def step(h, _):
            cs = pl.ds(pl.multiple_of(h * cols, cols), cols)
            y = st[slot_of(q + hop)]
            qh[q, :, cs] = (dot(y, wq[h, 0]).astype(BF) * scale).astype(BF)
            return 0

        lax.fori_loop(0, 2, step, 0)

    local[11].wait()
    local[12].wait()
    remote(qkv_h, wq.at[1 - core], w_send.at[0], w_recv.at[0], (band, mate)).wait_recv()
    from_mate(x + hop)
    project(x + hop)

    others = [lax.rem(x + k, xs) for k in range(1, xs)]
    for q in others:
        for u in range(halves):
            arrived(slot_of(q + hop), u)
            hand(q + hop, u).start()

    direct = ((x + hop - xs, below & (x >= xs - hop)), (x + hop + xs, above & (x < hop)))

    def take_direct(u):
        for i, (j, ok) in enumerate(direct):
            @pl.when(ok)
            def _(i=i, j=j):
                arrived(slot_of(j), u)
                for k in range(1, xs):
                    relay(i, k, j, u).start()

            @pl.when(ok & wanted(j))
            def _(j=j):
                hand(j, u).start()

    take_direct(0)
    query(x)
    for u in range(1, halves):
        take_direct(u)
    for k in range(1, xs):
        src = out_rows(same_core_src(head, k))
        remote(pout_h, src, ox_send.at[k - 1], ox_recv.at[k - 1], same_core(k)).wait_recv()
        out_pass(k).start()
    for q in others:
        from_mate(q + hop)
        project(q + hop)
        query(q)

    far = []
    for j in range(hop):
        far.append((j, below & (x != xs - hop + j)))
    for j in range(hop):
        far.append((xs + hop + j, above & (x != j)))
    for u in range(halves):
        for j, ok in far:
            @pl.when(ok)
            def _(j=j, u=u):
                arrived(slot_of(j), u)

            @pl.when(ok & wanted(j))
            def _(j=j, u=u):
                hand(j, u).start()
    for j, _ in far:
        from_mate(j)
        project(j)

    half_cols = qh.shape[2]

    def att_to(k):
        return remote(mine.at[k], got.at[x], a_send.at[k - 1], a_recv.at[k - 1], same_core(k))

    def window(q, dst):
        rs = pl.ds(pl.multiple_of((2 * q + core) * rows, rows), span)

        def step(j, _):
            cs = pl.ds(pl.multiple_of(j * wide, wide), wide)
            q2 = group_rows(qh[q, :, cs], GROUP, head_size)
            b = bias[q]
            scores = dot_t(q2, kp[rs, cs]) + jnp.concatenate([b] * GROUP, axis=0)
            o = dot(softmax_rows(scores), vp[rs, cs])
            mine[dst, :, cs] = group_merge(o, rows, GROUP, head_size).astype(BF)
            return 0

        steps = half_cols // wide
        lax.fori_loop(0, steps, step, 0, unroll=min(steps, 2))

    for k in range(1, xs):
        window(lax.rem(x + k, xs), k)
        att_to(k).start()
    window(x, 0)

    def out_block(q):
        return wo[pl.ds(pl.multiple_of(q * half_cols, half_cols), half_cols)]

    remote(pout_h, out_rows(mate), w_send.at[1], w_recv.at[1], (band, mate)).wait_recv()
    for k in range(1, xs):
        src = out_rows(same_core_src(mate, k))
        remote(pout_h, src, op_send.at[k - 1], op_recv.at[k - 1], (band, mate)).wait_recv()
    total = st[own].astype(F32) + dot(mine[0], out_block(x))
    for k in range(1, xs):
        src = lax.rem(x - k + xs, xs)
        remote(mine.at[k], got.at[src], a_send.at[k - 1], a_recv.at[k - 1],
               same_core(k)).wait_recv()
        total = total + dot(got[src], out_block(src))
    out[...] = total.astype(BF)

    @pl.when(jnp.logical_not(last))
    def _():
        up.wait_send()

    @pl.when(jnp.logical_not(first))
    def _():
        down.wait_send()

    qkv_mate.wait_send()
    out_mate.wait_send()
    for k in range(1, xs):
        out_cross(k).wait_send()
        out_pass(k).wait_send()
        att_to(k).wait_send()
    for u in range(halves):
        state_mate(u).wait_send()
        for k in range(1, xs):
            state_x(k, u).wait_send()
        for i, ok in enumerate((to_above, to_below)):
            @pl.when(ok)
            def _(i=i, u=u):
                state_v(i, u).wait_send()
        for q in others:
            hand(q + hop, u).wait_send()
        for i, (j, ok) in enumerate(direct):
            @pl.when(ok)
            def _(i=i, j=j, u=u):
                for k in range(1, xs):
                    relay(i, k, j, u).wait_send()

            @pl.when(ok & wanted(j))
            def _(j=j, u=u):
                hand(j, u).wait_send()
        for j, ok in far:
            @pl.when(ok & wanted(j))
            def _(j=j, u=u):
                hand(j, u).wait_send()


def local(nb, nh, grid_feat, mesh_feat, enc_query, enc_keyval, enc_out, proc_qkv, proc_out,
          tile_ids, key_counts):
    rows, dm = mesh_feat.shape
    grows = grid_feat.shape[0]
    tiles = grows // GT + 2 * HALO_TILES
    reach = HALFW // rows
    slots = nh + 2 * reach
    cols = proc_qkv.shape[2]
    xs = nh // 2
    nx = max(xs - 1, 1)
    halves = rows // MT
    dma = pltpu.SemaphoreType.DMA
    any_spec = pl.BlockSpec(memory_space=pl.ANY)
    smem = pl.BlockSpec(memory_space=pltpu.SMEM)
    return pl.pallas_call(
        functools.partial(kernel, nb, nh),
        out_shape=jax.ShapeDtypeStruct((rows, dm), BF),
        in_specs=[smem, smem] + [any_spec] * 7,
        out_specs=pl.BlockSpec(memory_space=pltpu.VMEM),
        scratch_shapes=[
            pltpu.VMEM((grows, dm), BF),
            pltpu.VMEM((2, HALO_TILES * GT, dm), BF),
            pltpu.VMEM(enc_keyval.shape, BF),
            pltpu.VMEM(enc_query.shape, BF),
            pltpu.VMEM(enc_out.shape, BF),
            pltpu.VMEM((rows, dm), BF),
            pltpu.VMEM((tiles, GT, 2 * dm), BF),
            pltpu.VMEM((2, 3, dm, cols), BF),
            pltpu.VMEM((nh * cols, dm), BF),
            pltpu.VMEM((slots, rows, dm), BF),
            pltpu.VMEM((rows, dm), BF),
            pltpu.VMEM((rows, dm), BF),
            pltpu.VMEM((xs, rows, 2 * cols), BF),
            pltpu.VMEM((slots * rows, 2 * cols), BF),
            pltpu.VMEM((slots * rows, 2 * cols), BF),
            pltpu.VMEM((xs, rows, 2 * cols), BF),
            pltpu.VMEM((xs, rows, 2 * cols), BF),
            pltpu.VMEM((xs, rows, (2 * reach + 1) * rows), F32),
            dma((13,)), dma((2,)), dma((2,)), dma((2,)), dma((2,)),
            dma((nx,)), dma((nx,)), dma((nx,)), dma((nx,)),
            dma((halves,)), dma((nx, halves)), dma((2, halves)), dma((2, nx, halves)),
            dma((slots // 2, halves)), dma((slots, halves)), dma((nx,)), dma((nx,)),
        ],
        compiler_params=pltpu.CompilerParams(
            collective_id=0, has_side_effects=True, vmem_limit_bytes=63 * 1024 * 1024),
    )(tile_ids, key_counts, grid_feat, mesh_feat, enc_query, enc_keyval, enc_out, proc_qkv,
      proc_out)


def solution(mesh):
    return jax.shard_map(
        functools.partial(local, mesh.shape["band"], mesh.shape["head"]),
        mesh=mesh,
        in_specs=(
            P(("band", "head"), None),
            P(("band", "head"), None),
            P(),
            P(),
            P(),
            P(None, None, "head"),
            P("head", None),
            P(("band", "head"), None),
            P(("band", "head")),
        ),
        out_specs=P(("band", "head"), None),
        check_vma=False,
    )
```

time: 84.6 us -> 61.5 us (0.73)
  the two profiles are of different devices: /device:TPU:25 before, /device:TPU:22 now
where the time goes in v2:
time: 61.5 us; the launch traced here: 61.3 us
  Pallas kernels  59.6 us (97%)
  local copies, waits for them, and re-layouts  1.67 us (3%)
    pallas_call x1, Pallas kernels, local(): pl.pallas_call(functools.partial(kernel, nb, nh), out_shape=jax.ShapeDtyp...  59.6 us
    unnamed x1, local copies, waits for them, and re-layouts  1.67 us

profile of v2, /device:TPU:22, one launch (start us, length us, event | category | flops | bytes accessed | tf_op | source)
XLA Modules:
  0.0 61.3 jit_solution(7665564306141481050)
XLA Ops:
  0.0 59.6 %shard_map.91 = bf16[128,1024]{1,0:T(8,128)(2,1)} custom-call(s32[2,8]{1,0:T(2,128)} %tid.1, s32[2]{0:T(128)} %cnt.1, bf16[2048,1024]{1,0:T(8,128)(2,1)} %grid.1, bf16[128,1024]{1,0:T(8,128)(2,1)} %feat_h.1, bf16[1024,1024]{1,0:T(8,128)(2,1)} %wquery_h.1, bf16[1024,2048]{1,0:T(8,128)(2,1)} %wkv_h.1, bf16[1024,1024]{1,0:T(8,128)(2,1)} %wenc_h.1, ...), custom_call_target="tpu_custom_call" | custom-call | tf_op jit(solution)/shard_map/pallas_call | solution.py:484
  59.7 1.7 %copy.11 = bf16[128,1024]{1,0:T(8,128)(2,1)} copy(bf16[128,1024]{1,0:T(8,128)(2,1)} %shard_map.91) | data formatting | bytes 524288

commit v3 on v2

--- a/solution.py
+++ b/solution.py
@@ -157,8 +157,6 @@
         src = out_rows(same_core_src(head, k))
         return remote(src, src, op_send.at[k - 1], op_recv.at[k - 1], (band, mate))
 
-    for k in range(1, xs):
-        out_cross(k).start()
     qkv_mate.start()
     out_mate.start()
 
@@ -362,9 +360,7 @@
     for u in range(1, halves):
         take_direct(u)
     for k in range(1, xs):
-        src = out_rows(same_core_src(head, k))
-        remote(pout_h, src, ox_send.at[k - 1], ox_recv.at[k - 1], same_core(k)).wait_recv()
-        out_pass(k).start()
+        out_cross(k).start()
     for q in others:
         from_mate(q + hop)
         project(q + hop)
@@ -411,6 +407,10 @@
     for k in range(1, xs):
         window(lax.rem(x + k, xs), k)
         att_to(k).start()
+    for k in range(1, xs):
+        src = out_rows(same_core_src(head, k))
+        remote(pout_h, src, ox_send.at[k - 1], ox_recv.at[k - 1], same_core(k)).wait_recv()
+        out_pass(k).start()
     window(x, 0)
 
     def out_block(q):

time: 61.5 us -> 64.9 us (1.055); the launches traced: 61.3 us -> 63.7 us
  Pallas kernels: 59.6 us -> 62 us
    pallas_call x1, Pallas kernels: 59.6 us -> 62 us  [local(): pl.pallas_call(functools.partial(kernel, nb, nh), out_shape=jax.ShapeDtyp...]
where the time goes in v3:
time: 64.9 us; the launch traced here: 63.7 us
  Pallas kernels  62 us (96%)
  local copies, waits for them, and re-layouts  1.67 us (3%)
    pallas_call x1, Pallas kernels, local(): pl.pallas_call(functools.partial(kernel, nb, nh), out_shape=jax.ShapeDtyp...  62 us
    unnamed x1, local copies, waits for them, and re-layouts  1.67 us

profile of v3, /device:TPU:22, one launch (start us, length us, event | category | flops | bytes accessed | tf_op | source)
XLA Modules:
  0.0 63.7 jit_solution(13975709033766141254)
XLA Ops:
  0.0 62.0 %shard_map.91 = bf16[128,1024]{1,0:T(8,128)(2,1)} custom-call(s32[2,8]{1,0:T(2,128)} %tid.1, s32[2]{0:T(128)} %cnt.1, bf16[2048,1024]{1,0:T(8,128)(2,1)} %grid.1, bf16[128,1024]{1,0:T(8,128)(2,1)} %feat_h.1, bf16[1024,1024]{1,0:T(8,128)(2,1)} %wquery_h.1, bf16[1024,2048]{1,0:T(8,128)(2,1)} %wkv_h.1, bf16[1024,1024]{1,0:T(8,128)(2,1)} %wenc_h.1, ...), custom_call_target="tpu_custom_call" | custom-call | tf_op jit(solution)/shard_map/pallas_call | solution.py:484
  62.1 1.7 %copy.11 = bf16[128,1024]{1,0:T(8,128)(2,1)} copy(bf16[128,1024]{1,0:T(8,128)(2,1)} %shard_map.91) | data formatting | bytes 524288

commit v4 on v2

--- a/solution.py
+++ b/solution.py
@@ -375,6 +375,11 @@
         far.append((j, below & (x != xs - hop + j)))
     for j in range(hop):
         far.append((xs + hop + j, above & (x != j)))
+    early = xs == hop == 2
+    if early:
+        for j in (x, x + xs + hop):
+            from_mate(j)
+            project(j)
     for u in range(halves):
         for j, ok in far:
             @pl.when(ok)
@@ -384,7 +389,7 @@
             @pl.when(ok & wanted(j))
             def _(j=j, u=u):
                 hand(j, u).start()
-    for j, _ in far:
+    for j in (xs - 1 - x, slots // 2 - 1 - x) if early else [j for j, _ in far]:
         from_mate(j)
         project(j)
 

time: 61.5 us -> 60.7 us (0.987)
  Pallas kernels: 59.6 us -> 58.8 us
    pallas_call x1, Pallas kernels: 59.6 us -> 58.8 us  [local(): pl.pallas_call(functools.partial(kernel, nb, nh), out_shape=jax.ShapeDtyp...]
where the time goes in v4:
time: 60.7 us; the launch traced here: 60.4 us
  Pallas kernels  58.8 us (97%)
  local copies, waits for them, and re-layouts  1.67 us (3%)
    pallas_call x1, Pallas kernels, local(): pl.pallas_call(functools.partial(kernel, nb, nh), out_shape=jax.ShapeDtyp...  58.8 us
    unnamed x1, local copies, waits for them, and re-layouts  1.67 us

profile of v4, /device:TPU:22, one launch (start us, length us, event | category | flops | bytes accessed | tf_op | source)
XLA Modules:
  0.0 60.4 jit_solution(15613072606622268054)
XLA Ops:
  0.0 58.8 %shard_map.91 = bf16[128,1024]{1,0:T(8,128)(2,1)} custom-call(s32[2,8]{1,0:T(2,128)} %tid.1, s32[2]{0:T(128)} %cnt.1, bf16[2048,1024]{1,0:T(8,128)(2,1)} %grid.1, bf16[128,1024]{1,0:T(8,128)(2,1)} %feat_h.1, bf16[1024,1024]{1,0:T(8,128)(2,1)} %wquery_h.1, bf16[1024,2048]{1,0:T(8,128)(2,1)} %wkv_h.1, bf16[1024,1024]{1,0:T(8,128)(2,1)} %wenc_h.1, ...), custom_call_target="tpu_custom_call" | custom-call | tf_op jit(solution)/shard_map/pallas_call | solution.py:489
  58.8 1.7 %copy.11 = bf16[128,1024]{1,0:T(8,128)(2,1)} copy(bf16[128,1024]{1,0:T(8,128)(2,1)} %shard_map.91) | data formatting | bytes 524288
